TPU v7x, 32 devices: a whole 2x2x4 slice. The times are simulated.
32 devices in a mesh: groups: 2 (over x), sky: 16 (over z, y, core).
Axes of the slice: x: 2, y: 2, z: 4, core: 2. Of those that a mesh axis runs over, the one named last changes fastest.
Arguments:
- image: bfloat16 [32, 512, 128], P(('groups', 'sky')), parts along dimension 0, may hold values from -6 to 6
- row_taps: bfloat16 [40, 31], replicated, may hold values from -1 to 1
- col_taps: bfloat16 [40, 31], replicated, may hold values from -1 to 1
- mix_coeff: float32 [32, 3, 40], P(('groups', 'sky')), parts along dimension 0, may hold values from -1 to 1
- shift_frac: float32 [32, 2], P(('groups', 'sky')), parts along dimension 0, may hold values from 0.05 to 0.95
- ccd_visit: int32 [32], P(('groups', 'sky')), parts along dimension 0, may hold values from 0 to 3
- visit_weight: bfloat16 [8], P('groups'), parts along dimension 0, may hold values from 0.25 to 4
- tile_block: int32 [2048], P(('groups', 'sky')), parts along dimension 0, may hold values from 0 to 255, as said below
- tile_offset: int32 [2048], P(('groups', 'sky')), parts along dimension 0, may hold values from 0 to 7
Outputs:
- coadd: float32 [4096, 128], P(('groups', 'sky')), parts along dimension 0
- weight_map: float32 [4096], P(('groups', 'sky')), parts along dimension 0
There are 2 independent parts, one for each index of `groups`. A program takes and returns all parts, laid end to end along the dimension named above; an argument that names none is the same for every part. Nothing has to cross between parts.
Inputs may be any that keep to these rules, and one draw needn't show every extreme that they name: `tile_block`: the owner of sky block b is device b // 16 of the sky axis. The 64 tiles of one window go to exactly 16 distinct owners, 4 tiles to each; at least four owners receive 4 tiles from every window.
All inputs are finite; a program needn't handle non-finite values.
Results may differ from a plain program's by a relative error of at most 0.0041.
Values may be sent and summed in bfloat16 or wider, within the bound.
A program may use at most 64 MiB of HBM per device.

v0:
```python
import jax
import jax.numpy as jnp
from jax import lax
from jax.sharding import PartitionSpec as P

TILE_R = 8
TILES_DEV = 64
BLK_DEV = 16


def shifted(value, axis, steps):
    count = lax.axis_size(axis)
    leading, last = (max(0, -steps), min(count, count - steps))
    return lax.ppermute(value, axis, [(source, source + steps) for source in range(leading, last)])


def lanczos_taps(fraction):
    positions = jnp.arange(-2, 4).astype(jnp.float32)
    offsets = positions[None, :] - fraction[:, None]
    angles = jnp.pi * offsets
    kernel = jnp.sin(angles) / angles * (jnp.sin(angles / 3.0) / (angles / 3.0))
    return kernel / jnp.sum(kernel, axis=1, keepdims=True)


def banded(taps_group, out_count):
    group_size, tap_count = taps_group.shape
    in_count = out_count + tap_count - 1
    zero_fill = jnp.zeros((group_size, in_count + 1 - tap_count), taps_group.dtype)
    row_pattern = jnp.concatenate([taps_group, zero_fill], axis=1)
    repeated = jnp.tile(row_pattern, (1, out_count))[:, : out_count * in_count]
    return repeated.reshape(group_size, out_count, in_count)


def match_window(window, row_taps, col_taps, coefficients):
    win_rows, win_cols = window.shape
    basis_count, tap_count = row_taps.shape
    half_taps = tap_count // 2
    row_block = min(128, win_rows)
    row_blocks = win_rows // row_block
    padded = jnp.pad(window, ((0, 0), (half_taps, half_taps)))
    col_slabs = jnp.stack([padded], axis=1)
    column_pos = (2.0 * jnp.arange(win_cols).astype(jnp.float32) + 1.0) / win_cols - 1.0
    row_pos = (2.0 * jnp.arange(win_rows).astype(jnp.float32) + 1.0) / win_rows - 1.0

    def add_group(group_index, running):
        first_basis = group_index * 2
        row_group = lax.dynamic_slice_in_dim(row_taps, first_basis, 2, 0)
        col_group = lax.dynamic_slice_in_dim(col_taps, first_basis, 2, 0)
        coef_group = lax.dynamic_slice_in_dim(coefficients, first_basis, 2, 1)
        across = jnp.einsum(
            "rbs,kcs->krbc", col_slabs, banded(row_group, 128), preferred_element_type=jnp.float32
        )
        smoothed = across.reshape(2, win_rows, win_cols).astype(jnp.bfloat16)
        rows_padded = jnp.pad(smoothed, ((0, 0), (half_taps, half_taps), (0, 0)))
        row_slabs = jnp.stack(
            [
                rows_padded[
                    :, block_index * row_block : block_index * row_block + row_block + 2 * half_taps
                ]
                for block_index in range(row_blocks)
            ],
            axis=1,
        )
        vertical = jnp.einsum(
            "krs,kbsc->kbrc",
            banded(col_group, row_block),
            row_slabs,
            preferred_element_type=jnp.float32,
        )
        vertical = vertical.reshape(2, win_rows, win_cols)
        weights = (
            coef_group[0][:, None, None]
            + coef_group[1][:, None, None] * column_pos[None, None, :]
            + coef_group[2][:, None, None] * row_pos[None, :, None]
        )
        return running + jnp.sum(weights * vertical, axis=0)

    return lax.fori_loop(
        0, basis_count // 2, add_group, jnp.zeros((win_rows, win_cols), jnp.float32)
    )


def warp_window(matched, fraction):
    win_rows, win_cols = matched.shape
    taps_across = lanczos_taps(fraction[1:2])[0]
    taps_down = lanczos_taps(fraction[0:1])[0]
    padded = jnp.pad(matched, ((0, 0), (2, 3)))
    spread = taps_across[0] * padded[:, 0:win_cols]
    for offset_index in range(1, 6):
        spread = (
            spread + taps_across[offset_index] * padded[:, offset_index : offset_index + win_cols]
        )
    padded = jnp.pad(spread, ((2, 3), (0, 0)))
    warped = taps_down[0] * padded[0:win_rows]
    for offset_index in range(1, 6):
        warped = warped + taps_down[offset_index] * padded[offset_index : offset_index + win_rows]
    return warped.astype(jnp.bfloat16)


def pack_slots(selector, tile_rows):
    return jnp.dot(
        selector.astype(jnp.bfloat16), tile_rows, preferred_element_type=jnp.float32
    ).astype(jnp.bfloat16)


def on_device(
    image,
    row_taps,
    col_taps,
    mix_coeff,
    shift_frac,
    ccd_visit,
    visit_weight,
    tile_block,
    tile_offset,
):
    win_cols = image.shape[2]
    matched = match_window(image[0], row_taps, col_taps, mix_coeff[0])
    warped = warp_window(matched, shift_frac[0])
    tile_count = TILES_DEV
    blocks_owned = BLK_DEV
    owned_rows = BLK_DEV * TILE_R
    sky_count = lax.axis_size("sky")
    capacity = max(2, tile_count // sky_count)
    slot_count = sky_count * capacity
    tile_rows = warped.reshape(tile_count, TILE_R * win_cols)
    tile_owner = tile_block // blocks_owned
    tile_local = tile_block - tile_owner * blocks_owned
    earlier = jnp.arange(tile_count)[None, :] < jnp.arange(tile_count)[:, None]
    tile_rank = jnp.sum((tile_owner[None, :] == tile_owner[:, None]) & earlier, axis=1)
    slot_ids = jnp.arange(slot_count)[:, None]
    visit_match = ccd_visit[:, None] == jnp.arange(visit_weight.shape[0])[None, :]
    own_weight = jnp.sum(
        jnp.where(visit_match, visit_weight[None, :], jnp.zeros((), jnp.bfloat16)), axis=1
    )
    main_select = slot_ids == (tile_owner * capacity + tile_rank)[None, :]
    send_main = pack_slots(main_select, tile_rows)
    filled = jnp.any(main_select, axis=1)
    starts = jnp.sum(
        jnp.where(main_select, (tile_local * TILE_R + tile_offset)[None, :], 0), axis=1
    )
    weights = jnp.where(filled, own_weight[0], jnp.zeros((), jnp.bfloat16))
    received, got_start, got_weight = (
        lax.all_to_all(send_main, "sky", split_axis=0, concat_axis=0, tiled=True),
        lax.all_to_all(starts, "sky", split_axis=0, concat_axis=0, tiled=True),
        lax.all_to_all(weights, "sky", split_axis=0, concat_axis=0, tiled=True),
    )
    slot_weight = got_weight.astype(jnp.float32)
    target = (got_start[:, None] + jnp.arange(TILE_R)[None, :]).reshape(-1)
    column_weight = jnp.repeat(got_weight, TILE_R)
    row_ids = jnp.arange(owned_rows + TILE_R)
    placement = jnp.where(
        row_ids[:, None] == target[None, :], column_weight[None, :], jnp.zeros((), jnp.bfloat16)
    )
    row_sums = jnp.dot(
        placement, received.reshape(-1, win_cols), preferred_element_type=jnp.float32
    )
    distance = row_ids[:, None] - got_start[None, :]
    covered = (distance >= 0) & (distance < TILE_R)
    totals = jnp.sum(jnp.where(covered, slot_weight[None, :], 0.0), axis=1)
    row_sums, totals = (row_sums, totals)
    carried_sums, carried_totals = shifted((row_sums[owned_rows:], totals[owned_rows:]), "sky", 1)
    sky_sum = jnp.concatenate(
        [row_sums[:TILE_R] + carried_sums, row_sums[TILE_R:owned_rows]], axis=0
    )
    weight_map = jnp.concatenate(
        [totals[:TILE_R] + carried_totals, totals[TILE_R:owned_rows]], axis=0
    )
    coadd = sky_sum / jnp.maximum(weight_map, 1.0)[:, None]
    return (coadd, weight_map)


def solution(mesh):
    return jax.shard_map(
        on_device,
        mesh=mesh,
        in_specs=(
            P(("groups", "sky"), None, None),
            P(),
            P(),
            P(("groups", "sky"), None, None),
            P(("groups", "sky"), None),
            P(("groups", "sky")),
            P("groups"),
            P(("groups", "sky")),
            P(("groups", "sky")),
        ),
        out_specs=(P(("groups", "sky"), None), P(("groups", "sky"))),
        check_vma=False,
    )
```

profile of v0, /device:TPU:10, one launch (start us, length us, event | category | flops | bytes accessed | tf_op | source)
XLA Modules:
  0.0 121.0 jit_solution(13972909325291598700)
XLA Ops:
  0.6 0.7 multiply_add_fusion.2
  2.3 0.6 copy-done.4
  2.9 0.6 fusion.39
  3.5 0.6 broadcast_select_fusion
  4.2 0.7 select_n.56
  4.9 6.4 %all-to-all-start.1 = ((bf16[16,4,1]{1,2,0:T(2,128)(2,1)}), bf16[16,4,1]{1,2,0:T(2,128)(2,1)S(1)}, u32[]{:S(2)}, u32[]{:S(2)}) async-start(bf16[16,4,1]{1,2,0:T(2,128)(2,1)} %select_n.56), calls=%async_computation.1 | async-start | bytes 16384 | tf_op jit(solution)/shard_map/all_to_all | solution.py:146
  11.3 0.7 copy-done.3
  12.1 1.0 copy.44
  13.2 0.6 copy-done.1
  13.9 61.1 %while.16 = (s32[]{:T(128)}, f32[512,128]{1,0:T(8,128)S(1)}, f32[3,40]{1,0:T(4,128)S(1)}, bf16[40,31]{1,0:T(8,128)(2,1)S(1)}, bf16[512,1,158]{0,2,1:T(8,128)(2,1...) while((s32[]{:T(128)}, f32[512,128]{1,0:T(8,128)S(1)}, ...), condition=%wide.region_8.9_spmd.clone, body=%wide.region_6.8_spmd.clone.sunk | while | flops 83917440 | bytes 4484617 | solution.py:78
  14.7 0.4 reshape.394
  15.6 0.4 reshape.395
  17.7 0.4 reshape.394
  18.6 0.4 reshape.395
  20.8 0.4 reshape.394
  21.7 0.4 reshape.395
  23.9 0.4 reshape.394
  24.8 0.4 reshape.395
  26.9 0.4 reshape.394
  27.8 0.4 reshape.395
  30.0 0.4 reshape.394
  30.9 0.4 reshape.395
  33.0 0.4 reshape.394
  33.9 0.4 reshape.395
  36.1 0.4 reshape.394
  37.0 0.4 reshape.395
  39.1 0.4 reshape.394
  40.0 0.4 reshape.395
  42.2 0.4 reshape.394
  43.1 0.4 reshape.395
  45.2 0.4 reshape.394
  46.1 0.4 reshape.395
  48.3 0.4 reshape.394
  49.2 0.4 reshape.395
  51.3 0.4 reshape.394
  52.2 0.4 reshape.395
  54.4 0.4 reshape.394
  55.3 0.4 reshape.395
  57.4 0.4 reshape.394
  58.3 0.4 reshape.395
  60.5 0.4 reshape.394
  66.6 0.4 reshape.394
  75.0 0.6 fusion.46
  75.6 1.3 %fusion.40 = f32[]{:T(128)} fusion(f32[]{:T(128)} %bitcast.4), kind=kLoop, calls=%fused_computation.90 | loop fusion | flops 53 | bytes 8 | tf_op jit(solution)/shard_map/reduce_sum | solution.py:22
  76.9 1.3 %fusion.41 = f32[1,6]{1,0:T(1,128)S(1)} fusion(f32[]{:T(128)} %fusion.40, f32[]{:T(128)} %bitcast.4), kind=kLoop, calls=%fused_computation.91 | loop fusion | flops 54 | bytes 32 | tf_op jit(solution)/shard_map/div | solution.py:22
  78.1 0.7 fusion.47
  78.8 1.3 %fusion.42 = f32[]{:T(128)} fusion(f32[]{:T(128)} %bitcast.2), kind=kLoop, calls=%fused_computation.92 | loop fusion | flops 53 | bytes 8 | tf_op jit(solution)/shard_map/reduce_sum | solution.py:22
  80.1 1.3 %fusion.43 = f32[1,6]{1,0:T(1,128)S(1)} fusion(f32[]{:T(128)} %fusion.42, f32[]{:T(128)} %bitcast.2), kind=kLoop, calls=%fused_computation.94 | loop fusion | flops 54 | bytes 32 | tf_op jit(solution)/shard_map/div | solution.py:22
  81.3 0.7 fusion.45
  82.0 4.1 %fusion.18 = f32[512,128]{1,0:T(8,128)S(1)} fusion(f32[512,128]{1,0:T(8,128)S(1)} %get-tuple-element.200, f32[]{:T(128)} %bitcast.12, f32[]{:T(128)} %bitcast.11, f32[]{:T(128)} %bitcast.10, f32[]{:T(128)} %bitcast.9, f32[]{:T(128)} %bitcast.8, f32[]{:T(128)} %bitcast.5), kind=kLoop, calls=%fused_computation.41 | loop fusion | flops 720896 | bytes 524312 | tf_op jit(solution)/shard_map/add | solution.py:91
  86.1 3.9 %add_convert_fusion = bf16[512,128]{1,0:T(8,128)(2,1)S(1)} fusion(f32[512,128]{1,0:T(8,128)S(1)} %fusion.18, f32[]{:T(128)} %bitcast.17, f32[]{:T(128)} %bitcast.16, f32[]{:T(128)} %bitcast.15, f32[]{:T(128)} %bitcast.14, f32[]{:T(128)} %bitcast.13, f32[]{:T(128)} %bitcast.3), kind=kLoop, calls=%fused_computation.46 | loop fusion | flops 786432 | bytes 393240 | tf_op jit(solution)/shard_map/convert_element_type | solution.py:97
  90.2 0.7 all_to_all.18
  90.9 6.0 %all-to-all-start = ((s32[16,4,1]{1,2,0:T(1,128)}), s32[16,4,1]{1,2,0:T(1,128)S(1)}, u32[]{:S(2)}, u32[]{:S(2)}) async-start(s32[16,4,1]{1,2,0:T(1,128)} %bitcast), calls=%async_computation | async-start | bytes 16384 | tf_op jit(solution)/shard_map/all_to_all | solution.py:145
  97.1 0.7 all_to_all.22
  98.1 3.8 %all-to-all-done = s32[16,4,1]{1,2,0:T(1,128)S(1)} async-done(((s32[16,4,1]{1,2,0:T(1,128)}), s32[16,4,1]{1,2,0:T(1,128)S(1)}, u32[]{:S(2)}, u32[]{:S(2)}) %all-to-all-start) | async-done | bytes 288 | tf_op jit(solution)/shard_map/all_to_all | solution.py:145
  101.9 4.8 %all-to-all-start.2 = ((bf16[16,4,1024]{2,1,0:T(4,128)(2,1)}), bf16[16,4,1024]{2,1,0:T(4,128)(2,1)S(1)}, u32[]{:S(2)}, u32[]{:S(2)}) async-start(bf16[16,4,1024]{2,1,0:T(4,128)(2,1)} %all_to_all.22), calls=%async_computation.2 | async-start | bytes 262144 | tf_op jit(solution)/shard_map/all_to_all | solution.py:144
  106.7 0.5 broadcast.334
  107.2 0.7 reduce.15
  108.4 2.0 %collective-permute-start.1 = (f32[8]{0:T(128)S(1)}, f32[8]{0:T(128)S(1)}, u32[]{:S(2)}, u32[]{:S(2)}) collective-permute-start(f32[8]{0:T(128)S(1)} %slice.226), channel_id=1, source_target_pairs={{0,1},{1,2},{2,3},{3,4},{4,5},{5,6},{6,7},{7,8},{8,9},{9,10},{10,1... | collective-permute-start | bytes 104 | tf_op jit(solution)/shard_map/ppermute | solution.py:14
  110.4 3.7 %collective-permute-done.1 = f32[8]{0:T(128)S(1)} collective-permute-done((f32[8]{0:T(128)S(1)}, f32[8]{0:T(128)S(1)}, u32[]{:S(2)}, u32[]{:S(2)}) %collective-permute-start.1) | collective-permute-done | bytes 64 | tf_op jit(solution)/shard_map/ppermute | solution.py:14
  114.4 1.9 %collective-permute-start = (f32[8,128]{1,0:T(8,128)S(1)}, f32[8,128]{1,0:T(8,128)S(1)}, u32[]{:S(2)}, u32[]{:S(2)}) collective-permute-start(f32[8,128]{1,0:T(8,128)S(1)} %slice.242), channel_id=1, source_target_pairs={{0,1},{1,2},{2,3},{3,4},{4,5},{5,6},{6,7},{7,8},{8,9},{9,10},{10,1... | collective-permute-start | bytes 12296 | tf_op jit(solution)/shard_map/ppermute | solution.py:14
  116.3 0.6 broadcast_maximum_fusion
  116.9 3.3 %collective-permute-done = f32[8,128]{1,0:T(8,128)S(1)} collective-permute-done((f32[8,128]{1,0:T(8,128)S(1)}, f32[8,128]{1,0:T(8,128)S(1)}, u32[]{:S(2)}, u32[]{:S(2)}) %collective-permute-start) | collective-permute-done | bytes 4128 | tf_op jit(solution)/shard_map/ppermute | solution.py:14
  120.2 0.7 maximum_divide_fusion
  (445 shorter events, 47.4 us)
Async XLA Ops:
  2.3 0.7 copy-start.4
  4.9 7.1 %copy-start = (bf16[40,31]{0,1:T(8,128)(2,1)S(1)}, bf16[40,31]{0,1:T(8,128)(2,1)}, u32[]{:S(2)}) copy-start(bf16[40,31]{0,1:T(8,128)(2,1)} %param.12) | copy-start | bytes 7444
  4.9 86.0 %all-to-all-start.1 = ((bf16[16,4,1]{1,2,0:T(2,128)(2,1)}), bf16[16,4,1]{1,2,0:T(2,128)(2,1)S(1)}, u32[]{:S(2)}, u32[]{:S(2)}) async-start(bf16[16,4,1]{1,2,0:T(2,128)(2,1)} %select_n.56), calls=%async_computation.1 | async-start | bytes 16384 | tf_op jit(solution)/shard_map/all_to_all | solution.py:146
  11.3 0.7 copy-start.3
  13.1 0.7 copy-start.1
  13.9 61.1 %copy-start.2 = (f32[1,2]{1,0:T(1,128)S(1)}, f32[1,2]{1,0:T(1,128)}, u32[]{:S(2)}) copy-start(f32[1,2]{1,0:T(1,128)} %param.15) | copy-start | bytes 28
  90.9 11.0 %all-to-all-start = ((s32[16,4,1]{1,2,0:T(1,128)}), s32[16,4,1]{1,2,0:T(1,128)S(1)}, u32[]{:S(2)}, u32[]{:S(2)}) async-start(s32[16,4,1]{1,2,0:T(1,128)} %bitcast), calls=%async_computation | async-start | bytes 16384 | tf_op jit(solution)/shard_map/all_to_all | solution.py:145
  101.9 12.3 %all-to-all-start.2 = ((bf16[16,4,1024]{2,1,0:T(4,128)(2,1)}), bf16[16,4,1024]{2,1,0:T(4,128)(2,1)S(1)}, u32[]{:S(2)}, u32[]{:S(2)}) async-start(bf16[16,4,1024]{2,1,0:T(4,128)(2,1)} %all_to_all.22), calls=%async_computation.2 | async-start | bytes 262144 | tf_op jit(solution)/shard_map/all_to_all | solution.py:144
  108.4 5.8 %collective-permute-start.1 = (f32[8]{0:T(128)S(1)}, f32[8]{0:T(128)S(1)}, u32[]{:S(2)}, u32[]{:S(2)}) collective-permute-start(f32[8]{0:T(128)S(1)} %slice.226), channel_id=1, source_target_pairs={{0,1},{1,2},{2,3},{3,4},{4,5},{5,6},{6,7},{7,8},{8,9},{9,10},{10,1... | collective-permute-start | bytes 104 | tf_op jit(solution)/shard_map/ppermute | solution.py:14
  114.4 5.8 %collective-permute-start = (f32[8,128]{1,0:T(8,128)S(1)}, f32[8,128]{1,0:T(8,128)S(1)}, u32[]{:S(2)}, u32[]{:S(2)}) collective-permute-start(f32[8,128]{1,0:T(8,128)S(1)} %slice.242), channel_id=1, source_target_pairs={{0,1},{1,2},{2,3},{3,4},{4,5},{5,6},{6,7},{7,8},{8,9},{9,10},{10,1... | collective-permute-start | bytes 12296 | tf_op jit(solution)/shard_map/ppermute | solution.py:14
where the time goes:
time: 122 us; the launch traced here: 121 us
  local copies, waits for them, and re-layouts  51.9 us (43%)
  other arithmetic  22 us (18%)
  starting transfers between devices  21.2 us (17%)
  matrix products  10.8 us (9%)
  waiting for transfers between devices  10.8 us (9%)
  loops' own time  2.8 us (2%)
  between operations  1.48 us (1%)
    another operation x80, local copies, waits for them, and re-layouts, banded(): repeated = jnp.tile(row_pattern, (1, out_count))[:, :out_count * in_count]  16.1 us
    reshape x40, local copies, waits for them, and re-layouts, banded(): return repeated.reshape(group_size, out_count, in_count)  15.9 us
    ppermute x2, waiting for transfers between devices, shifted(): lax.ppermute(value, axis, [(source, source + steps) for source in range(l...  7.05 us
    all_to_all x1, starting transfers between devices, on_device(): lax.all_to_all(weights, 'sky', split_axis=0, concat_axis=0, tiled=True)  6.43 us
    dot_general x20, matrix products, add_group(): jnp.einsum('krs,kbsc->kbrc', banded(col_group, row_block), row_slabs, pre...  6.25 us
    all_to_all x1, starting transfers between devices, on_device(): lax.all_to_all(starts, 'sky', split_axis=0, concat_axis=0, tiled=True)  6.01 us
    all_to_all x1, starting transfers between devices, on_device(): lax.all_to_all(send_main, 'sky', split_axis=0, concat_axis=0, tiled=True)  4.84 us
    another operation x20, local copies, waits for them, and re-layouts, add_group(): jnp.stack([rows_padded[:, block_index * row_block:block_index * row_block...  4.57 us
  transfers between devices with their start and end apart: 5, of which 3 were waited for; matrix products, arithmetic and copies ran while one was open for 64% of the time, Pallas kernels for 0%

commit v1 on v0

v1 whole, which is shorter than its diff:
```python
import functools

import jax
import jax.numpy as jnp
from jax import lax
from jax.experimental import pallas as pl
from jax.experimental.pallas import tpu as pltpu
from jax.sharding import PartitionSpec as P

TILE_R = 8
BLK_DEV = 16
LANES = 128
F32 = jnp.float32
BF16 = jnp.bfloat16


def iota(shape, axis):
    return lax.broadcasted_iota(jnp.int32, shape, axis)


def dot(lhs, rhs):
    return jnp.dot(lhs, rhs, preferred_element_type=F32)


def onehot(mask):
    return jnp.where(mask, 1.0, 0.0).astype(BF16)


def lanczos(fraction, rows):
    lane = iota((rows, LANES), 1)
    offsets = (lane - 2).astype(F32) - fraction
    offsets = jnp.where(lane < 6, offsets, 0.5)
    angles = jnp.pi * offsets
    thirds = angles / 3.0
    kernel = jnp.sin(angles) / angles * (jnp.sin(thirds) / thirds)
    kernel = jnp.where(lane < 6, kernel, 0.0)
    return kernel / jnp.sum(kernel, axis=1, keepdims=True)


def kernel(
    sky,
    image_ref,
    row_taps_ref,
    col_taps_ref,
    mix_ref,
    shift_ref,
    visit_ref,
    visit_weight_ref,
    block_ref,
    offset_ref,
    coadd_ref,
    weight_ref,
    xpad,
    lhs,
    rhs_hi,
    rhs_lo,
    taps2d,
    spread_pad,
    meta_send,
    meta_recv,
    data_send,
    data_recv,
    meta_ssem,
    meta_rsem,
    data_ssem,
    data_rsem,
):
    me = lax.axis_index("sky")
    win_rows, win_cols = image_ref.shape
    basis, tap_count = row_taps_ref.shape
    half = tap_count // 2
    tiles = block_ref.shape[1]
    cap = max(2, tiles // sky)
    span = cap * TILE_R
    owned_rows = BLK_DEV * TILE_R
    blk_shift = BLK_DEV.bit_length() - 1

    barrier = pltpu.get_barrier_semaphore()

    def greet(step, carry):
        pl.semaphore_signal(
            barrier,
            inc=1,
            device_id={"sky": lax.rem(me + step, sky)},
            device_id_type=pl.DeviceIdType.MESH,
        )
        return carry

    lax.fori_loop(1, sky, greet, 0)

    block = block_ref[...]
    owner_i = lax.shift_right_logical(block, blk_shift)
    start_row = ((block - owner_i * BLK_DEV) * TILE_R + offset_ref[...]).astype(F32)
    owner_row = owner_i.astype(F32)
    eye = iota((tiles, tiles), 0) == iota((tiles, tiles), 1)
    column = lambda row: jnp.sum(
        jnp.where(eye, jnp.broadcast_to(row, (tiles, tiles)), 0.0), axis=1, keepdims=True
    )
    owner_col = column(owner_row)
    start_col = column(start_row)
    same = owner_col == owner_row
    below = iota((tiles, tiles), 0) < iota((tiles, tiles), 1)
    above = iota((tiles, tiles), 1) < iota((tiles, tiles), 0)
    rank_row = jnp.sum(jnp.where(same & below, 1.0, 0.0), axis=0, keepdims=True)
    rank_col = jnp.sum(jnp.where(same & above, 1.0, 0.0), axis=1, keepdims=True)
    visits = visit_weight_ref.shape[1]
    own_weight = jnp.sum(
        jnp.where(
            iota((1, visits), 1) == visit_ref[0, 0], visit_weight_ref[...].astype(F32), 0.0
        ),
        axis=1,
        keepdims=True,
    )

    per_group = LANES // span
    sub = iota((sky * TILE_R, tiles), 0)
    to_owner = onehot(lax.shift_right_logical(sub, 3).astype(F32) == owner_row)
    lane = iota((tiles, LANES), 1)
    mine = lax.div(lane, jnp.int32(span)) == lax.rem(me, per_group)
    slot_rank = lax.div(lax.rem(lane, jnp.int32(span)), jnp.int32(TILE_R)).astype(F32)
    landing = start_col + (lax.rem(lane, jnp.int32(TILE_R)) + 1).astype(F32)
    landing = jnp.where(mine & (slot_rank == rank_col), landing, 0.0)
    targets = dot(to_owner, landing.astype(BF16))
    lane8 = iota((sky * TILE_R, LANES), 1)
    sub8 = lax.rem(iota((sky * TILE_R, LANES), 0), jnp.int32(TILE_R))
    weight8 = jnp.broadcast_to(own_weight, (sky * TILE_R, LANES))
    tile_lanes = lax.div(lane8, jnp.int32(span)) == lax.rem(me, per_group)
    spill_lanes = lax.div(lane8, jnp.int32(16)) == lax.rem(me, 8)
    header = jnp.where(
        sub8 == 0,
        targets,
        jnp.where(
            sub8 == 1,
            jnp.where(tile_lanes, weight8, 0.0),
            jnp.where((sub8 == 2) & spill_lanes, weight8, 0.0),
        ),
    )
    row_in = lax.rem(sub, jnp.int32(TILE_R)).astype(F32)
    before = lax.shift_right_logical(sub, 3).astype(F32) - 1.0
    over = onehot(
        (before == owner_row) & (start_row > row_in + float(owned_rows - TILE_R))
    )
    covered = dot(over, jnp.ones((tiles, LANES), BF16))
    meta_send[:, 0:TILE_R, :] = header.reshape(sky, TILE_R, LANES)
    meta_send[:, TILE_R:, :] = covered.reshape(sky, TILE_R, LANES)

    pl.semaphore_wait(barrier, sky - 1)

    def message(send, recv, ssem, rsem, step):
        to = lax.rem(me + step, sky)
        return pltpu.make_async_remote_copy(
            src_ref=send.at[to],
            dst_ref=recv.at[me],
            send_sem=ssem.at[step],
            recv_sem=rsem.at[step],
            device_id={"sky": to},
            device_id_type=pl.DeviceIdType.MESH,
        )

    def start_meta(step, carry):
        message(meta_send, meta_recv, meta_ssem, meta_rsem, step).start()
        return carry

    lax.fori_loop(1, sky, start_meta, 0)
    meta_recv[pl.ds(me, 1)] = meta_send[pl.ds(me, 1)]

    flip = onehot(
        iota((tap_count, LANES), 1)
        == lax.rem(half - iota((tap_count, LANES), 0) + LANES, jnp.int32(LANES))
    )
    rows_flipped = dot(row_taps_ref[...], flip)
    eye_k = onehot(iota((basis, basis), 0) == iota((basis, basis), 1))
    col_t = lax.dot_general(
        col_taps_ref[...], eye_k, (((0,), (0,)), ((), ())), preferred_element_type=F32
    )
    taps2d[...] = jnp.zeros_like(taps2d)
    for term in range(3):
        taps2d[term, 0:tap_count, :] = jnp.dot(
            col_t * mix_ref[term : term + 1, :],
            rows_flipped,
            preferred_element_type=F32,
            precision=lax.Precision.HIGHEST,
        )

    xpad[...] = jnp.zeros_like(xpad)
    xpad[pl.ds(16, win_rows), :] = image_ref[...].astype(F32)

    square = (win_cols, win_cols)
    band = jnp.abs(iota(square, 0) - iota(square, 1)) <= half
    column_pos = (2.0 * iota((1, win_cols), 1).astype(F32) + 1.0) / win_cols - 1.0

    def toeplitz(term, tap):
        row = jnp.broadcast_to(taps2d[term, pl.ds(tap, 1), :], square)
        return pltpu.roll(row, 0, 1, stride=1, stride_axis=0)

    def put(block_index, tap):
        here = pl.ds(block_index * win_cols, win_cols)
        both = (
            jnp.where(band, toeplitz(0, tap) + column_pos * toeplitz(1, tap), 0.0),
            jnp.where(band, toeplitz(2, tap), 0.0),
        )
        for side, value in enumerate(both):
            top = value.astype(BF16)
            rhs_hi[here, side * win_cols : (side + 1) * win_cols] = top
            rhs_lo[here, side * win_cols : (side + 1) * win_cols] = (
                value - top.astype(F32)
            ).astype(BF16)

    def build(tap, carry):
        put(2 * tap, tap)
        put(2 * tap + 1, tap + 16)
        return carry

    lax.fori_loop(0, 16, build, 0)
    for tap in range(16):
        moved = xpad[pl.ds(tap + 16 - half, win_rows + 16), :].astype(BF16)
        lhs[:, tap * 256 : tap * 256 + 128] = moved[0:win_rows]
        lhs[:, tap * 256 + 128 : tap * 256 + 256] = moved[16 : win_rows + 16]
    both = dot(lhs[...], rhs_hi[...]) + dot(lhs[...], rhs_lo[...])
    row_pos = (2.0 * iota((win_rows, win_cols), 0).astype(F32) + 1.0) / win_rows - 1.0
    matched = both[:, 0:win_cols] + row_pos * both[:, win_cols:]

    across = lanczos(shift_ref[0, 1], 8)
    down = lanczos(shift_ref[0, 0], 8)
    lanes = iota((win_rows, win_cols), 1)
    spread = across[0:1, 2:3] * matched
    for m in (-2, -1, 1, 2, 3):
        moved = pltpu.roll(matched, (-m) % win_cols, 1)
        keep = (lanes + m >= 0) & (lanes + m < win_cols)
        spread = spread + across[0:1, m + 2 : m + 3] * jnp.where(keep, moved, 0.0)
    spread_pad[0:8, :] = jnp.zeros((8, win_cols), F32)
    spread_pad[win_rows + 8 : win_rows + 16, :] = jnp.zeros((8, win_cols), F32)
    spread_pad[8 : win_rows + 8, :] = spread
    warped = down[0:1, 0:1] * spread_pad[pl.ds(6, win_rows), :]
    for m in range(-1, 4):
        warped = warped + down[0:1, m + 2 : m + 3] * spread_pad[pl.ds(8 + m, win_rows), :]
    warped = warped.astype(BF16)

    wide = tiles * TILE_R
    widen = onehot(
        iota((tiles, wide), 0) == lax.shift_right_logical(iota((tiles, wide), 1), 3)
    )
    in_tile = lax.rem(iota((1, wide), 1), jnp.int32(TILE_R)).astype(F32)
    spread8 = lambda row: dot(jnp.broadcast_to(row, (8, tiles)).astype(BF16), widen)[0:1, :]
    slot_lane = spread8(owner_row * cap + rank_row) * TILE_R + in_tile
    past = spread8(start_row) + in_tile - float(owned_rows)
    spill_lane = jnp.where(past >= 0.0, (spread8(owner_row) + 1.0) * TILE_R + past, -1.0)
    sent = sky * span
    pick = onehot(iota((sent, wide), 0).astype(F32) == slot_lane)
    data_send[:, 0:span, :] = dot(pick, warped).astype(BF16).reshape(sky, span, win_cols)
    pick = onehot(iota((sky * TILE_R, wide), 0).astype(F32) == spill_lane)
    spill = dot(pick, warped)
    spill_hi = spill.astype(BF16).astype(F32)
    spill_lo = spill - spill_hi
    data_send[:, span:, :] = jnp.concatenate(
        [spill_hi.reshape(sky, TILE_R, win_cols), spill_lo.reshape(sky, TILE_R, win_cols)],
        axis=1,
    ).astype(BF16)

    def start_data(step, carry):
        message(data_send, data_recv, data_ssem, data_rsem, step).start()
        return carry

    lax.fori_loop(1, sky, start_data, 0)
    data_recv[pl.ds(me, 1)] = data_send[pl.ds(me, 1)]

    def wait_meta(step, carry):
        copy = message(meta_send, meta_recv, meta_ssem, meta_rsem, step)
        copy.wait_send()
        copy.wait_recv()
        return carry

    lax.fori_loop(1, sky, wait_meta, 0)

    owned = (owned_rows, LANES)
    row_id = (iota(owned, 0) + 1).astype(F32)
    places = []
    total = jnp.zeros((owned_rows, win_cols), F32)
    ones = jnp.ones((LANES, win_cols), BF16)
    for group in range(sky // per_group):
        head = jnp.sum(
            meta_recv[group * per_group : (group + 1) * per_group, 0:TILE_R, :], axis=0
        )
        place = jnp.where(head[0:1, :] == row_id, head[1:2, :], 0.0).astype(BF16)
        places.append(place)
        total = total + dot(place, ones)
    spill_places = []
    same_row = lax.rem(iota(owned, 1), jnp.int32(TILE_R)) == iota(owned, 0)
    for group in range(sky // 8):
        head = jnp.sum(meta_recv[group * 8 : (group + 1) * 8, 0:TILE_R, :], axis=0)
        place = jnp.where(same_row, head[2:3, :], 0.0).astype(BF16)
        spill_places.append(place)
        count = meta_recv[group * 8 : (group + 1) * 8, TILE_R:, :]
        count = jnp.concatenate([count, jnp.zeros_like(count)], axis=1)
        total = total + dot(place, count.reshape(LANES, LANES).astype(BF16))
    diagonal = iota(owned, 0) == iota(owned, 1)
    weight_ref[...] = jnp.sum(jnp.where(diagonal, total, 0.0), axis=0, keepdims=True)

    def wait_data(step, carry):
        copy = message(data_send, data_recv, data_ssem, data_rsem, step)
        copy.wait_send()
        copy.wait_recv()
        return carry

    lax.fori_loop(1, sky, wait_data, 0)
    sums = jnp.zeros((owned_rows, win_cols), F32)
    for group, place in enumerate(places):
        part = data_recv[group * per_group : (group + 1) * per_group, 0:span, :]
        sums = sums + dot(place, part.reshape(LANES, win_cols))
    for group, place in enumerate(spill_places):
        part = data_recv[group * 8 : (group + 1) * 8, span:, :]
        sums = sums + dot(place, part.reshape(LANES, win_cols))
    coadd_ref[...] = sums / jnp.maximum(total, 1.0)


def on_device(
    image,
    row_taps,
    col_taps,
    mix_coeff,
    shift_frac,
    ccd_visit,
    visit_weight,
    tile_block,
    tile_offset,
):
    sky = lax.axis_size("sky")
    win_rows, win_cols = image.shape[1:]
    tiles = tile_block.shape[0]
    span = max(2, tiles // sky) * TILE_R
    owned_rows = BLK_DEV * TILE_R
    vmem = pl.BlockSpec(memory_space=pltpu.VMEM)
    smem = pl.BlockSpec(memory_space=pltpu.SMEM)
    coadd, weight_map = pl.pallas_call(
        functools.partial(kernel, sky),
        out_shape=(
            jax.ShapeDtypeStruct((owned_rows, win_cols), F32),
            jax.ShapeDtypeStruct((1, owned_rows), F32),
        ),
        in_specs=[vmem, vmem, vmem, vmem, smem, smem, vmem, vmem, vmem],
        out_specs=(vmem, vmem),
        scratch_shapes=[
            pltpu.VMEM((win_rows + 32, win_cols), F32),
            pltpu.VMEM((win_rows, 32 * win_cols), BF16),
            pltpu.VMEM((32 * win_cols, 2 * win_cols), BF16),
            pltpu.VMEM((32 * win_cols, 2 * win_cols), BF16),
            pltpu.VMEM((3, 32, LANES), F32),
            pltpu.VMEM((win_rows + 16, win_cols), F32),
            pltpu.VMEM((sky, 2 * TILE_R, LANES), F32),
            pltpu.VMEM((sky, 2 * TILE_R, LANES), F32),
            pltpu.VMEM((sky, span + 16, win_cols), BF16),
            pltpu.VMEM((sky, span + 16, win_cols), BF16),
            pltpu.SemaphoreType.DMA((sky,)),
            pltpu.SemaphoreType.DMA((sky,)),
            pltpu.SemaphoreType.DMA((sky,)),
            pltpu.SemaphoreType.DMA((sky,)),
        ],
        compiler_params=pltpu.CompilerParams(collective_id=0, has_side_effects=True),
        name="coadd",
    )(
        image[0],
        row_taps,
        col_taps,
        mix_coeff[0],
        shift_frac,
        ccd_visit.reshape(1, 1),
        visit_weight.reshape(1, -1),
        tile_block.reshape(1, -1),
        tile_offset.reshape(1, -1),
    )
    return coadd, weight_map.reshape(owned_rows)


def solution(mesh):
    return jax.shard_map(
        on_device,
        mesh=mesh,
        in_specs=(
            P(("groups", "sky"), None, None),
            P(),
            P(),
            P(("groups", "sky"), None, None),
            P(("groups", "sky"), None),
            P(("groups", "sky")),
            P("groups"),
            P(("groups", "sky")),
            P(("groups", "sky")),
        ),
        out_specs=(P(("groups", "sky"), None), P(("groups", "sky"))),
        check_vma=False,
    )
```

time: 122 us -> 25.2 us (0.21)
  the two profiles are of different devices: /device:TPU:10 before, /device:TPU:0 now
where the time goes in v1:
time: 25.2 us; the launch traced here: 24.9 us
  Pallas kernels  19 us (75%)
  local copies, waits for them, and re-layouts  4.61 us (18%)
  between operations  1.33 us (5%)
    pallas_call x1, Pallas kernels, on_device(): pl.pallas_call(functools.partial(kernel, sky), out_shape=(jax.ShapeDtypeS...  19 us
    unnamed x13, local copies, waits for them, and re-layouts  4.61 us

profile of v1, /device:TPU:0, one launch (start us, length us, event | category | flops | bytes accessed | tf_op | source)
XLA Modules:
  0.0 24.9 jit_solution(5174591612598784569)
XLA Ops:
  0.6 0.0 copy-start
  1.3 0.0 copy-start.2
  1.3 0.7 %copy-done.2 = f32[1,3,40]{2,0,1:T(1,128)S(1)} copy-done((f32[1,3,40]{2,0,1:T(1,128)S(1)}, f32[1,3,40]{2,0,1:T(1,128)}, u32[]{:S(2)}) %copy-start.2) | copy-done | bytes 504
  2.0 0.6 %copy.15 = f32[1,3,40]{2,1,0:T(4,128)} copy(f32[1,3,40]{2,0,1:T(1,128)S(1)} %copy-done.2) | data formatting | bytes 960
  2.5 0.0 copy-done
  2.5 0.0 copy-start.1
  2.5 0.7 %copy.11.row_taps_ref = bf16[40,31]{1,0:T(8,128)(2,1)} copy(bf16[40,31]{0,1:T(8,128)(2,1)S(1)} %copy-done) | data formatting | bytes 4960 | tf_op args[1]
  3.2 0.0 copy-done.1
  3.2 0.7 %copy.12.col_taps_ref = bf16[40,31]{1,0:T(8,128)(2,1)} copy(bf16[40,31]{0,1:T(8,128)(2,1)S(1)} %copy-done.1) | data formatting | bytes 4960 | tf_op args[2]
  3.9 19.0 %coadd.1 = (f32[128,128]{1,0:T(8,128)}, f32[1,128]{1,0:T(1,128)}) custom-call(bf16[512,128]{1,0:T(8,128)(2,1)} %bitcast.10, bf16[40,31]{1,0:T(8,128)(2,1)} %copy.11.row_taps_ref, bf16[40,31]{1,0:T(8,128)(2,1)} %copy.12.col_taps_ref, f32[3,40]{1,0:T(4,128)} %bitcast.11, f32[1,2]{1,0:T(1,128)} %shift_ref.1, s32[1,1]{1,0:T(1,128)} %bitcast.9.visit_ref, ...), custom_call_target="tpu_custom_call" | custom-call | tf_op jit(solution)/shard_map/coadd/pallas_call | solution.py:334
  22.9 0.0 copy-start.3
  22.9 1.5 %copy.19 = f32[128,128]{1,0:T(8,128)} copy(f32[128,128]{1,0:T(8,128)} %get-tuple-element.8) | data formatting | bytes 131072
  24.4 0.0 copy-done.3
  24.4 0.5 %copy.20 = f32[128]{0:T(128)} copy(f32[128]{0:T(128)S(1)} %bitcast.15) | data formatting | bytes 1024
Async XLA Ops:
  0.6 1.9 %copy-start = (bf16[40,31]{0,1:T(8,128)(2,1)S(1)}, bf16[40,31]{0,1:T(8,128)(2,1)}, u32[]{:S(2)}) copy-start(bf16[40,31]{0,1:T(8,128)(2,1)} %param.10) | copy-start | bytes 7444
  1.3 0.7 %copy-start.2 = (f32[1,3,40]{2,0,1:T(1,128)S(1)}, f32[1,3,40]{2,0,1:T(1,128)}, u32[]{:S(2)}) copy-start(f32[1,3,40]{2,0,1:T(1,128)} %param.12) | copy-start | bytes 1444
  2.5 0.7 %copy-start.1 = (bf16[40,31]{0,1:T(8,128)(2,1)S(1)}, bf16[40,31]{0,1:T(8,128)(2,1)}, u32[]{:S(2)}) copy-start(bf16[40,31]{0,1:T(8,128)(2,1)} %param.11) | copy-start | bytes 7444
  22.9 1.5 %copy-start.3 = (f32[1,128]{1,0:T(1,128)S(1)}, f32[1,128]{1,0:T(1,128)}, u32[]{:S(2)}) copy-start(f32[1,128]{1,0:T(1,128)} %get-tuple-element.5) | copy-start | bytes 1540

commit v2 on v1

--- a/solution.py
+++ b/solution.py
@@ -10,6 +10,7 @@
 TILE_R = 8
 BLK_DEV = 16
 LANES = 128
+STEPS = 4
 F32 = jnp.float32
 BF16 = jnp.bfloat16
 
@@ -26,8 +27,8 @@
     return jnp.where(mask, 1.0, 0.0).astype(BF16)
 
 
-def lanczos(fraction, rows):
-    lane = iota((rows, LANES), 1)
+def lanczos(fraction):
+    lane = iota((1, LANES), 1)
     offsets = (lane - 2).astype(F32) - fraction
     offsets = jnp.where(lane < 6, offsets, 0.5)
     angles = jnp.pi * offsets
@@ -48,12 +49,11 @@
     visit_weight_ref,
     block_ref,
     offset_ref,
-    coadd_ref,
-    weight_ref,
+    result_ref,
     xpad,
     lhs,
-    rhs_hi,
-    rhs_lo,
+    rhs,
+    pick,
     taps2d,
     spread_pad,
     meta_send,
@@ -67,7 +67,7 @@
 ):
     me = lax.axis_index("sky")
     win_rows, win_cols = image_ref.shape
-    basis, tap_count = row_taps_ref.shape
+    tap_count, basis = row_taps_ref.shape
     half = tap_count // 2
     tiles = block_ref.shape[1]
     cap = max(2, tiles // sky)
@@ -106,7 +106,7 @@
     visits = visit_weight_ref.shape[1]
     own_weight = jnp.sum(
         jnp.where(
-            iota((1, visits), 1) == visit_ref[0, 0], visit_weight_ref[...].astype(F32), 0.0
+            iota((1, visits), 1) == visit_ref[...], visit_weight_ref[...].astype(F32), 0.0
         ),
         axis=1,
         keepdims=True,
@@ -151,11 +151,23 @@
         return pltpu.make_async_remote_copy(
             src_ref=send.at[to],
             dst_ref=recv.at[me],
-            send_sem=ssem.at[step],
-            recv_sem=rsem.at[step],
+            send_sem=ssem,
+            recv_sem=rsem,
             device_id={"sky": to},
             device_id_type=pl.DeviceIdType.MESH,
         )
+
+    def wait_all(send, recv, ssem, rsem):
+        copy = pltpu.make_async_remote_copy(
+            src_ref=send.at[pl.ds(0, sky - 1)],
+            dst_ref=recv.at[pl.ds(0, sky - 1)],
+            send_sem=ssem,
+            recv_sem=rsem,
+            device_id={"sky": lax.rem(me + 1, sky)},
+            device_id_type=pl.DeviceIdType.MESH,
+        )
+        copy.wait_send()
+        copy.wait_recv()
 
     def start_meta(step, carry):
         message(meta_send, meta_recv, meta_ssem, meta_rsem, step).start()
@@ -168,15 +180,14 @@
         iota((tap_count, LANES), 1)
         == lax.rem(half - iota((tap_count, LANES), 0) + LANES, jnp.int32(LANES))
     )
-    rows_flipped = dot(row_taps_ref[...], flip)
-    eye_k = onehot(iota((basis, basis), 0) == iota((basis, basis), 1))
-    col_t = lax.dot_general(
-        col_taps_ref[...], eye_k, (((0,), (0,)), ((), ())), preferred_element_type=F32
-    )
+    rows_flipped = lax.dot_general(
+        row_taps_ref[...], flip, (((0,), (0,)), ((), ())), preferred_element_type=F32
+    )
+    col_t = col_taps_ref[...].astype(F32)
     taps2d[...] = jnp.zeros_like(taps2d)
     for term in range(3):
         taps2d[term, 0:tap_count, :] = jnp.dot(
-            col_t * mix_ref[term : term + 1, :],
+            col_t * mix_ref[term],
             rows_flipped,
             preferred_element_type=F32,
             precision=lax.Precision.HIGHEST,
@@ -200,28 +211,46 @@
             jnp.where(band, toeplitz(2, tap), 0.0),
         )
         for side, value in enumerate(both):
-            top = value.astype(BF16)
-            rhs_hi[here, side * win_cols : (side + 1) * win_cols] = top
-            rhs_lo[here, side * win_cols : (side + 1) * win_cols] = (
-                value - top.astype(F32)
-            ).astype(BF16)
-
-    def build(tap, carry):
-        put(2 * tap, tap)
-        put(2 * tap + 1, tap + 16)
-        return carry
-
-    lax.fori_loop(0, 16, build, 0)
-    for tap in range(16):
-        moved = xpad[pl.ds(tap + 16 - half, win_rows + 16), :].astype(BF16)
-        lhs[:, tap * 256 : tap * 256 + 128] = moved[0:win_rows]
-        lhs[:, tap * 256 + 128 : tap * 256 + 256] = moved[16 : win_rows + 16]
-    both = dot(lhs[...], rhs_hi[...]) + dot(lhs[...], rhs_lo[...])
+            rhs[here, side * win_cols : (side + 1) * win_cols] = value.astype(BF16)
+
+    wide = tiles * TILE_R
+    widen = onehot(
+        iota((tiles, wide), 0) == lax.shift_right_logical(iota((tiles, wide), 1), 3)
+    )
+    in_tile = lax.rem(iota((1, wide), 1), jnp.int32(TILE_R)).astype(F32)
+    spread8 = lambda row: dot(jnp.broadcast_to(row, (8, tiles)).astype(BF16), widen)[0:1, :]
+    slot_lane = spread8(owner_row * cap + rank_row) * TILE_R + in_tile
+    past = spread8(start_row) + in_tile - float(owned_rows)
+    spill_lane = jnp.where(past >= 0.0, (spread8(owner_row) + 1.0) * TILE_R + past, -1.0)
+    sent = sky * span
+
+    def build(first, last):
+        for tap in range(first, last):
+            put(2 * tap, tap)
+            put(2 * tap + 1, tap + 16)
+            moved = xpad[pl.ds(tap + 16 - half, win_rows + 16), :].astype(BF16)
+            lhs[:, tap * 256 : tap * 256 + 128] = moved[0:win_rows]
+            lhs[:, tap * 256 + 128 : tap * 256 + 256] = moved[16 : win_rows + 16]
+
+    depth = 16 // STEPS
+    both = None
+    build(0, depth)
+    for step in range(STEPS):
+        if step + 1 < STEPS:
+            build((step + 1) * depth, (step + 2) * depth)
+        else:
+            pick[0:sent, :] = onehot(iota((sent, wide), 0).astype(F32) == slot_lane)
+            pick[sent:, :] = onehot(
+                iota((sky * TILE_R, wide), 0).astype(F32) == spill_lane
+            )
+        inner = slice(step * depth * 256, (step + 1) * depth * 256)
+        term = dot(lhs[:, inner], rhs[inner, :])
+        both = term if both is None else both + term
     row_pos = (2.0 * iota((win_rows, win_cols), 0).astype(F32) + 1.0) / win_rows - 1.0
     matched = both[:, 0:win_cols] + row_pos * both[:, win_cols:]
 
-    across = lanczos(shift_ref[0, 1], 8)
-    down = lanczos(shift_ref[0, 0], 8)
+    across = lanczos(shift_ref[0:1, 1:2])
+    down = lanczos(shift_ref[0:1, 0:1])
     lanes = iota((win_rows, win_cols), 1)
     spread = across[0:1, 2:3] * matched
     for m in (-2, -1, 1, 2, 3):
@@ -236,20 +265,9 @@
         warped = warped + down[0:1, m + 2 : m + 3] * spread_pad[pl.ds(8 + m, win_rows), :]
     warped = warped.astype(BF16)
 
-    wide = tiles * TILE_R
-    widen = onehot(
-        iota((tiles, wide), 0) == lax.shift_right_logical(iota((tiles, wide), 1), 3)
-    )
-    in_tile = lax.rem(iota((1, wide), 1), jnp.int32(TILE_R)).astype(F32)
-    spread8 = lambda row: dot(jnp.broadcast_to(row, (8, tiles)).astype(BF16), widen)[0:1, :]
-    slot_lane = spread8(owner_row * cap + rank_row) * TILE_R + in_tile
-    past = spread8(start_row) + in_tile - float(owned_rows)
-    spill_lane = jnp.where(past >= 0.0, (spread8(owner_row) + 1.0) * TILE_R + past, -1.0)
-    sent = sky * span
-    pick = onehot(iota((sent, wide), 0).astype(F32) == slot_lane)
-    data_send[:, 0:span, :] = dot(pick, warped).astype(BF16).reshape(sky, span, win_cols)
-    pick = onehot(iota((sky * TILE_R, wide), 0).astype(F32) == spill_lane)
-    spill = dot(pick, warped)
+    packed = dot(pick[...], warped)
+    data_send[:, 0:span, :] = packed[0:sent].astype(BF16).reshape(sky, span, win_cols)
+    spill = packed[sent:]
     spill_hi = spill.astype(BF16).astype(F32)
     spill_lo = spill - spill_hi
     data_send[:, span:, :] = jnp.concatenate(
@@ -264,13 +282,7 @@
     lax.fori_loop(1, sky, start_data, 0)
     data_recv[pl.ds(me, 1)] = data_send[pl.ds(me, 1)]
 
-    def wait_meta(step, carry):
-        copy = message(meta_send, meta_recv, meta_ssem, meta_rsem, step)
-        copy.wait_send()
-        copy.wait_recv()
-        return carry
-
-    lax.fori_loop(1, sky, wait_meta, 0)
+    wait_all(meta_send, meta_recv, meta_ssem, meta_rsem)
 
     owned = (owned_rows, LANES)
     row_id = (iota(owned, 0) + 1).astype(F32)
@@ -294,15 +306,11 @@
         count = jnp.concatenate([count, jnp.zeros_like(count)], axis=1)
         total = total + dot(place, count.reshape(LANES, LANES).astype(BF16))
     diagonal = iota(owned, 0) == iota(owned, 1)
-    weight_ref[...] = jnp.sum(jnp.where(diagonal, total, 0.0), axis=0, keepdims=True)
-
-    def wait_data(step, carry):
-        copy = message(data_send, data_recv, data_ssem, data_rsem, step)
-        copy.wait_send()
-        copy.wait_recv()
-        return carry
-
-    lax.fori_loop(1, sky, wait_data, 0)
+    result_ref[owned_rows:, :] = jnp.broadcast_to(
+        jnp.sum(jnp.where(diagonal, total, 0.0), axis=0, keepdims=True), (8, LANES)
+    )
+
+    wait_all(data_send, data_recv, data_ssem, data_rsem)
     sums = jnp.zeros((owned_rows, win_cols), F32)
     for group, place in enumerate(places):
         part = data_recv[group * per_group : (group + 1) * per_group, 0:span, :]
@@ -310,7 +318,13 @@
     for group, place in enumerate(spill_places):
         part = data_recv[group * 8 : (group + 1) * 8, span:, :]
         sums = sums + dot(place, part.reshape(LANES, win_cols))
-    coadd_ref[...] = sums / jnp.maximum(total, 1.0)
+    result_ref[0:owned_rows, :] = sums / jnp.maximum(total, 1.0)
+
+
+def hand_over(result_ref, coadd_ref, weight_ref):
+    owned_rows = coadd_ref.shape[0]
+    coadd_ref[...] = result_ref[0:owned_rows, :]
+    weight_ref[...] = result_ref[owned_rows : owned_rows + 1, :]
 
 
 def on_device(
@@ -330,44 +344,50 @@
     span = max(2, tiles // sky) * TILE_R
     owned_rows = BLK_DEV * TILE_R
     vmem = pl.BlockSpec(memory_space=pltpu.VMEM)
-    smem = pl.BlockSpec(memory_space=pltpu.SMEM)
-    coadd, weight_map = pl.pallas_call(
+    result = pl.pallas_call(
         functools.partial(kernel, sky),
-        out_shape=(
-            jax.ShapeDtypeStruct((owned_rows, win_cols), F32),
-            jax.ShapeDtypeStruct((1, owned_rows), F32),
-        ),
-        in_specs=[vmem, vmem, vmem, vmem, smem, smem, vmem, vmem, vmem],
-        out_specs=(vmem, vmem),
+        out_shape=pltpu.VMEM((owned_rows + 8, win_cols), F32),
+        in_specs=[vmem] * 9,
+        out_specs=vmem,
         scratch_shapes=[
             pltpu.VMEM((win_rows + 32, win_cols), F32),
             pltpu.VMEM((win_rows, 32 * win_cols), BF16),
             pltpu.VMEM((32 * win_cols, 2 * win_cols), BF16),
-            pltpu.VMEM((32 * win_cols, 2 * win_cols), BF16),
+            pltpu.VMEM((sky * (span + TILE_R), tiles * TILE_R), BF16),
             pltpu.VMEM((3, 32, LANES), F32),
             pltpu.VMEM((win_rows + 16, win_cols), F32),
             pltpu.VMEM((sky, 2 * TILE_R, LANES), F32),
             pltpu.VMEM((sky, 2 * TILE_R, LANES), F32),
             pltpu.VMEM((sky, span + 16, win_cols), BF16),
             pltpu.VMEM((sky, span + 16, win_cols), BF16),
-            pltpu.SemaphoreType.DMA((sky,)),
-            pltpu.SemaphoreType.DMA((sky,)),
-            pltpu.SemaphoreType.DMA((sky,)),
-            pltpu.SemaphoreType.DMA((sky,)),
+            pltpu.SemaphoreType.DMA,
+            pltpu.SemaphoreType.DMA,
+            pltpu.SemaphoreType.DMA,
+            pltpu.SemaphoreType.DMA,
         ],
         compiler_params=pltpu.CompilerParams(collective_id=0, has_side_effects=True),
         name="coadd",
     )(
         image[0],
-        row_taps,
-        col_taps,
-        mix_coeff[0],
+        row_taps.T,
+        col_taps.T,
+        mix_coeff.transpose(1, 0, 2),
         shift_frac,
         ccd_visit.reshape(1, 1),
         visit_weight.reshape(1, -1),
         tile_block.reshape(1, -1),
         tile_offset.reshape(1, -1),
     )
+    coadd, weight_map = pl.pallas_call(
+        hand_over,
+        out_shape=(
+            jax.ShapeDtypeStruct((owned_rows, win_cols), F32),
+            jax.ShapeDtypeStruct((1, owned_rows), F32),
+        ),
+        in_specs=[vmem],
+        out_specs=(vmem, vmem),
+        name="hand_over",
+    )(pltpu.with_memory_space_constraint(result, pltpu.VMEM))
     return coadd, weight_map.reshape(owned_rows)
 
 

time: 25.2 us -> 16.3 us (0.65)
  local copies, waits for them, and re-layouts: 4.61 us -> 0 us
  Pallas kernels: 19 us -> 14.9 us
    unnamed x13 -> x0, local copies, waits for them, and re-layouts: 4.61 us -> none
    pallas_call x1 -> x2, Pallas kernels: 19 us -> 14.9 us  [the longest x1 14.2 us: on_device(): pl.pallas_call(functools.partial(kernel, sky), out_shape=pltpu.VMEM((owne...]
where the time goes in v2:
time: 16.3 us; the launch traced here: 16.2 us
  Pallas kernels  14.9 us (91%)
  between operations  1.29 us (8%)
    pallas_call x1, Pallas kernels, on_device(): pl.pallas_call(functools.partial(kernel, sky), out_shape=pltpu.VMEM((owne...  14.2 us
    pallas_call x1, Pallas kernels, on_device(): pl.pallas_call(hand_over, out_shape=(jax.ShapeDtypeStruct((owned_rows, wi...  0.64 us

profile of v2, /device:TPU:0, one launch (start us, length us, event | category | flops | bytes accessed | tf_op | source)
XLA Modules:
  0.0 16.2 jit_solution(18293959090087329914)
XLA Ops:
  1.3 14.2 %coadd.1.result_ref = f32[136,128]{1,0:T(8,128)S(1)} custom-call(bf16[512,128]{1,0:T(8,128)(2,1)} %bitcast.10, bf16[31,40]{1,0:T(8,128)(2,1)} %bitcast.11, bf16[31,40]{1,0:T(8,128)(2,1)} %bitcast.12, f32[3,1,40]{2,1,0:T(1,128)} %bitcast.13, f32[1,2]{1,0:T(1,128)} %shift_ref.1, s32[1,1]{1,0:T(1,128)} %bitcast.9.visit_ref, bf16[1,4]{1,0:T(2,128)(2,1)} %bitcast.14, ...), custom_call_target="tpu_custom_call" | custom-call | tf_op jit(solution)/shard_map/coadd/pallas_call | solution.py:347
  15.5 0.6 %hand_over.1 = (f32[128,128]{1,0:T(8,128)}, f32[1,128]{1,0:T(1,128)}) custom-call(f32[136,128]{1,0:T(8,128)S(1)} %coadd.1.result_ref), custom_call_target="tpu_custom_call" | custom-call | tf_op jit(solution)/shard_map/hand_over/pallas_call | solution.py:381

commit v3 on v2

--- a/solution.py
+++ b/solution.py
@@ -55,6 +55,7 @@
     rhs,
     pick,
     taps2d,
+    acc,
     spread_pad,
     meta_send,
     meta_recv,
@@ -113,40 +114,32 @@
     )
 
     per_group = LANES // span
+    spill_group = min(LANES // TILE_R, sky)
     sub = iota((sky * TILE_R, tiles), 0)
-    to_owner = onehot(lax.shift_right_logical(sub, 3).astype(F32) == owner_row)
+    owner_of = lax.shift_right_logical(sub, 3).astype(F32)
     lane = iota((tiles, LANES), 1)
     mine = lax.div(lane, jnp.int32(span)) == lax.rem(me, per_group)
     slot_rank = lax.div(lax.rem(lane, jnp.int32(span)), jnp.int32(TILE_R)).astype(F32)
-    landing = start_col + (lax.rem(lane, jnp.int32(TILE_R)) + 1).astype(F32)
-    landing = jnp.where(mine & (slot_rank == rank_col), landing, 0.0)
-    targets = dot(to_owner, landing.astype(BF16))
+    in_eight = lax.rem(lane, jnp.int32(TILE_R)).astype(F32)
+    landing = jnp.where(mine & (slot_rank == rank_col), start_col + in_eight + 1.0, 0.0)
+    targets = dot(onehot(owner_of == owner_row), landing.astype(BF16))
+    mine = lax.div(lane, jnp.int32(TILE_R)) == lax.rem(me, spill_group)
+    cover = onehot(mine & (start_col > in_eight + float(owned_rows - TILE_R)))
+    covered = dot(onehot(owner_of - 1.0 == owner_row), cover)
     lane8 = iota((sky * TILE_R, LANES), 1)
     sub8 = lax.rem(iota((sky * TILE_R, LANES), 0), jnp.int32(TILE_R))
     weight8 = jnp.broadcast_to(own_weight, (sky * TILE_R, LANES))
     tile_lanes = lax.div(lane8, jnp.int32(span)) == lax.rem(me, per_group)
-    spill_lanes = lax.div(lane8, jnp.int32(16)) == lax.rem(me, 8)
-    header = jnp.where(
-        sub8 == 0,
-        targets,
-        jnp.where(
-            sub8 == 1,
-            jnp.where(tile_lanes, weight8, 0.0),
-            jnp.where((sub8 == 2) & spill_lanes, weight8, 0.0),
-        ),
-    )
-    row_in = lax.rem(sub, jnp.int32(TILE_R)).astype(F32)
-    before = lax.shift_right_logical(sub, 3).astype(F32) - 1.0
-    over = onehot(
-        (before == owner_row) & (start_row > row_in + float(owned_rows - TILE_R))
-    )
-    covered = dot(over, jnp.ones((tiles, LANES), BF16))
-    meta_send[:, 0:TILE_R, :] = header.reshape(sky, TILE_R, LANES)
-    meta_send[:, TILE_R:, :] = covered.reshape(sky, TILE_R, LANES)
-
-    pl.semaphore_wait(barrier, sky - 1)
-
-    def message(send, recv, ssem, rsem, step):
+    spill_lanes = lax.div(lane8, jnp.int32(TILE_R)) == lax.rem(me, spill_group)
+    header = jnp.where((sub8 == 1) & tile_lanes, weight8, 0.0)
+    header = jnp.where((sub8 == 2) & spill_lanes, weight8, header)
+    header = jnp.where(sub8 == 3, covered * weight8, header)
+    header = jnp.where(sub8 == 0, targets, header)
+    meta_send[...] = header.reshape(sky, TILE_R, LANES)
+
+    def message(send, recv, ssem, rsem, turn):
+        away = lax.div(turn, 2)
+        step = sky // 2 + jnp.where(lax.rem(turn, 2) == 1, away, -away)
         to = lax.rem(me + step, sky)
         return pltpu.make_async_remote_copy(
             src_ref=send.at[to],
@@ -173,45 +166,62 @@
         message(meta_send, meta_recv, meta_ssem, meta_rsem, step).start()
         return carry
 
-    lax.fori_loop(1, sky, start_meta, 0)
-    meta_recv[pl.ds(me, 1)] = meta_send[pl.ds(me, 1)]
-
-    flip = onehot(
-        iota((tap_count, LANES), 1)
-        == lax.rem(half - iota((tap_count, LANES), 0) + LANES, jnp.int32(LANES))
-    )
-    rows_flipped = lax.dot_general(
-        row_taps_ref[...], flip, (((0,), (0,)), ((), ())), preferred_element_type=F32
-    )
-    col_t = col_taps_ref[...].astype(F32)
-    taps2d[...] = jnp.zeros_like(taps2d)
-    for term in range(3):
-        taps2d[term, 0:tap_count, :] = jnp.dot(
-            col_t * mix_ref[term],
-            rows_flipped,
+    def flip(place):
+        tap = iota((tap_count, LANES), 0)
+        return onehot(
+            iota((tap_count, LANES), 1)
+            == lax.rem(half + place - tap + LANES, jnp.int32(LANES))
+        )
+
+    def flipped(place):
+        return lax.dot_general(
+            row_taps_ref[...], flip(place), (((0,), (0,)), ((), ())), preferred_element_type=F32
+        )
+
+    def mixed(term, taps):
+        return jnp.dot(
+            col_taps_ref[...].astype(F32) * mix_ref[term],
+            taps,
             preferred_element_type=F32,
             precision=lax.Precision.HIGHEST,
         )
 
+    near, far = flipped(0), flipped(LANES // 2)
+    taps2d[...] = jnp.zeros_like(taps2d)
+    taps2d[0, 0:tap_count, :] = mixed(0, near) + mixed(2, far)
+    taps2d[1, 0:tap_count, :] = mixed(1, near)
+
     xpad[...] = jnp.zeros_like(xpad)
     xpad[pl.ds(16, win_rows), :] = image_ref[...].astype(F32)
 
     square = (win_cols, win_cols)
+    wrapped = lax.rem(iota(square, 1) + LANES // 2, jnp.int32(LANES))
     band = jnp.abs(iota(square, 0) - iota(square, 1)) <= half
-    column_pos = (2.0 * iota((1, win_cols), 1).astype(F32) + 1.0) / win_cols - 1.0
-
-    def toeplitz(term, tap):
-        row = jnp.broadcast_to(taps2d[term, pl.ds(tap, 1), :], square)
-        return pltpu.roll(row, 0, 1, stride=1, stride_axis=0)
+    far_band = jnp.abs(iota(square, 0) - wrapped) <= half
+    eight = (TILE_R, LANES)
+    signed = lax.rem(iota(eight, 1) + LANES // 2, jnp.int32(LANES)) - LANES // 2
+    column_pos = (2.0 * signed.astype(F32) + 1.0) / win_cols - 1.0
 
     def put(block_index, tap):
         here = pl.ds(block_index * win_cols, win_cols)
-        both = (
-            jnp.where(band, toeplitz(0, tap) + column_pos * toeplitz(1, tap), 0.0),
-            jnp.where(band, toeplitz(2, tap), 0.0),
-        )
-        for side, value in enumerate(both):
-            rhs[here, side * win_cols : (side + 1) * win_cols] = value.astype(BF16)
+        fixed, slope = (
+            pltpu.roll(
+                jnp.broadcast_to(taps2d[term, tap : tap + 1, :], eight),
+                0,
+                1,
+                stride=1,
+                stride_axis=0,
+            )
+            for term in range(2)
+        )
+        fixed = fixed + column_pos * slope
+        rows = []
+        for first in range(0, win_cols, TILE_R):
+            value = fixed + (2.0 * first / win_cols) * slope
+            rows.append(pltpu.roll(value, first, 1) if first else value)
+        value = jnp.concatenate(rows, axis=0)
+        rhs[here, 0:win_cols] = jnp.where(band, value, 0.0).astype(BF16)
+        rhs[here, win_cols:] = jnp.where(far_band, value, 0.0).astype(BF16)
 
     wide = tiles * TILE_R
     widen = onehot(
@@ -233,7 +243,6 @@
             lhs[:, tap * 256 + 128 : tap * 256 + 256] = moved[16 : win_rows + 16]
 
     depth = 16 // STEPS
-    both = None
     build(0, depth)
     for step in range(STEPS):
         if step + 1 < STEPS:
@@ -245,35 +254,46 @@
             )
         inner = slice(step * depth * 256, (step + 1) * depth * 256)
         term = dot(lhs[:, inner], rhs[inner, :])
-        both = term if both is None else both + term
-    row_pos = (2.0 * iota((win_rows, win_cols), 0).astype(F32) + 1.0) / win_rows - 1.0
-    matched = both[:, 0:win_cols] + row_pos * both[:, win_cols:]
+        acc[...] = term if step == 0 else acc[...] + term
+
+    pl.semaphore_wait(barrier, sky - 1)
+    lax.fori_loop(1, sky, start_meta, 0)
+    meta_recv[pl.ds(me, 1)] = meta_send[pl.ds(me, 1)]
 
     across = lanczos(shift_ref[0:1, 1:2])
     down = lanczos(shift_ref[0:1, 0:1])
-    lanes = iota((win_rows, win_cols), 1)
-    spread = across[0:1, 2:3] * matched
-    for m in (-2, -1, 1, 2, 3):
-        moved = pltpu.roll(matched, (-m) % win_cols, 1)
-        keep = (lanes + m >= 0) & (lanes + m < win_cols)
-        spread = spread + across[0:1, m + 2 : m + 3] * jnp.where(keep, moved, 0.0)
+    lane = iota((1, win_cols), 1)
+    chunk = min(64, win_rows)
     spread_pad[0:8, :] = jnp.zeros((8, win_cols), F32)
     spread_pad[win_rows + 8 : win_rows + 16, :] = jnp.zeros((8, win_cols), F32)
-    spread_pad[8 : win_rows + 8, :] = spread
-    warped = down[0:1, 0:1] * spread_pad[pl.ds(6, win_rows), :]
-    for m in range(-1, 4):
-        warped = warped + down[0:1, m + 2 : m + 3] * spread_pad[pl.ds(8 + m, win_rows), :]
-    warped = warped.astype(BF16)
+    across_taps = [
+        jnp.where((lane + m >= 0) & (lane + m < win_cols), across[0:1, m + 2 : m + 3], 0.0)
+        for m in range(-2, 4)
+    ]
+    down_taps = [
+        jnp.broadcast_to(down[0:1, m + 2 : m + 3], (1, win_cols)) for m in range(-2, 4)
+    ]
+    for first in range(0, win_rows, chunk):
+        here = slice(first, first + chunk)
+        row_pos = (iota((chunk, win_cols), 0) + first).astype(F32)
+        row_pos = (2.0 * row_pos + 1.0) / win_rows - 1.0
+        sloped = pltpu.roll(acc[here, win_cols:], LANES // 2, 1)
+        matched = acc[here, 0:win_cols] + row_pos * sloped
+        spread = across_taps[2] * matched
+        for m in (-2, -1, 1, 2, 3):
+            spread = spread + across_taps[m + 2] * pltpu.roll(matched, (-m) % win_cols, 1)
+        spread_pad[first + 8 : first + 8 + chunk, :] = spread
+    warped = []
+    for first in range(0, win_rows, chunk):
+        value = down_taps[0] * spread_pad[pl.ds(first + 6, chunk), :]
+        for m in range(-1, 4):
+            value = value + down_taps[m + 2] * spread_pad[pl.ds(first + 8 + m, chunk), :]
+        warped.append(value.astype(BF16))
+    warped = jnp.concatenate(warped, axis=0)
 
     packed = dot(pick[...], warped)
     data_send[:, 0:span, :] = packed[0:sent].astype(BF16).reshape(sky, span, win_cols)
-    spill = packed[sent:]
-    spill_hi = spill.astype(BF16).astype(F32)
-    spill_lo = spill - spill_hi
-    data_send[:, span:, :] = jnp.concatenate(
-        [spill_hi.reshape(sky, TILE_R, win_cols), spill_lo.reshape(sky, TILE_R, win_cols)],
-        axis=1,
-    ).astype(BF16)
+    data_send[:, span:, :] = packed[sent:].reshape(sky, TILE_R, win_cols).astype(BF16)
 
     def start_data(step, carry):
         message(data_send, data_recv, data_ssem, data_rsem, step).start()
@@ -291,20 +311,23 @@
     ones = jnp.ones((LANES, win_cols), BF16)
     for group in range(sky // per_group):
         head = jnp.sum(
-            meta_recv[group * per_group : (group + 1) * per_group, 0:TILE_R, :], axis=0
+            meta_recv[group * per_group : (group + 1) * per_group], axis=0
         )
         place = jnp.where(head[0:1, :] == row_id, head[1:2, :], 0.0).astype(BF16)
         places.append(place)
         total = total + dot(place, ones)
     spill_places = []
     same_row = lax.rem(iota(owned, 1), jnp.int32(TILE_R)) == iota(owned, 0)
-    for group in range(sky // 8):
-        head = jnp.sum(meta_recv[group * 8 : (group + 1) * 8, 0:TILE_R, :], axis=0)
-        place = jnp.where(same_row, head[2:3, :], 0.0).astype(BF16)
-        spill_places.append(place)
-        count = meta_recv[group * 8 : (group + 1) * 8, TILE_R:, :]
-        count = jnp.concatenate([count, jnp.zeros_like(count)], axis=1)
-        total = total + dot(place, count.reshape(LANES, LANES).astype(BF16))
+    here_row = lax.rem(iota(eight, 1), jnp.int32(TILE_R)) == iota(eight, 0)
+    first_rows = jnp.zeros(eight, F32)
+    for group in range(sky // spill_group):
+        head = jnp.sum(meta_recv[group * spill_group : (group + 1) * spill_group], axis=0)
+        spill_places.append(jnp.where(same_row, head[2:3, :], 0.0).astype(BF16))
+        count = jnp.sum(jnp.where(here_row, head[3:4, :], 0.0), axis=1, keepdims=True)
+        first_rows = first_rows + jnp.broadcast_to(count, eight)
+    total = total + jnp.concatenate(
+        [first_rows, jnp.zeros((owned_rows - TILE_R, LANES), F32)], axis=0
+    )
     diagonal = iota(owned, 0) == iota(owned, 1)
     result_ref[owned_rows:, :] = jnp.broadcast_to(
         jnp.sum(jnp.where(diagonal, total, 0.0), axis=0, keepdims=True), (8, LANES)
@@ -316,8 +339,9 @@
         part = data_recv[group * per_group : (group + 1) * per_group, 0:span, :]
         sums = sums + dot(place, part.reshape(LANES, win_cols))
     for group, place in enumerate(spill_places):
-        part = data_recv[group * 8 : (group + 1) * 8, span:, :]
-        sums = sums + dot(place, part.reshape(LANES, win_cols))
+        part = data_recv[group * spill_group : (group + 1) * spill_group, span:, :]
+        part = part.astype(F32).reshape(spill_group * TILE_R, win_cols).astype(BF16)
+        sums = sums + dot(place[:, 0 : spill_group * TILE_R], part)
     result_ref[0:owned_rows, :] = sums / jnp.maximum(total, 1.0)
 
 
@@ -354,12 +378,13 @@
             pltpu.VMEM((win_rows, 32 * win_cols), BF16),
             pltpu.VMEM((32 * win_cols, 2 * win_cols), BF16),
             pltpu.VMEM((sky * (span + TILE_R), tiles * TILE_R), BF16),
-            pltpu.VMEM((3, 32, LANES), F32),
+            pltpu.VMEM((2, 32, LANES), F32),
+            pltpu.VMEM((win_rows, 2 * win_cols), F32),
             pltpu.VMEM((win_rows + 16, win_cols), F32),
-            pltpu.VMEM((sky, 2 * TILE_R, LANES), F32),
-            pltpu.VMEM((sky, 2 * TILE_R, LANES), F32),
-            pltpu.VMEM((sky, span + 16, win_cols), BF16),
-            pltpu.VMEM((sky, span + 16, win_cols), BF16),
+            pltpu.VMEM((sky, TILE_R, LANES), F32),
+            pltpu.VMEM((sky, TILE_R, LANES), F32),
+            pltpu.VMEM((sky, span + TILE_R, win_cols), BF16),
+            pltpu.VMEM((sky, span + TILE_R, win_cols), BF16),
             pltpu.SemaphoreType.DMA,
             pltpu.SemaphoreType.DMA,
             pltpu.SemaphoreType.DMA,

time: 16.3 us -> 16.7 us (1.025)
  Pallas kernels: 14.9 us -> 15.3 us
    pallas_call x1, Pallas kernels: 14.2 us -> 14.6 us  [on_device(): pl.pallas_call(functools.partial(kernel, sky), out_shape=pltpu.VMEM((owne...]
where the time goes in v3:
time: 16.7 us; the launch traced here: 16.5 us
  Pallas kernels  15.3 us (92%)
  between operations  1.29 us (8%)
    pallas_call x1, Pallas kernels, on_device(): pl.pallas_call(functools.partial(kernel, sky), out_shape=pltpu.VMEM((owne...  14.6 us
    pallas_call x1, Pallas kernels, on_device(): pl.pallas_call(hand_over, out_shape=(jax.ShapeDtypeStruct((owned_rows, wi...  0.64 us

profile of v3, /device:TPU:0, one launch (start us, length us, event | category | flops | bytes accessed | tf_op | source)
XLA Modules:
  0.0 16.5 jit_solution(15318324449155246130)
XLA Ops:
  1.3 14.6 %coadd.1.result_ref = f32[136,128]{1,0:T(8,128)S(1)} custom-call(bf16[512,128]{1,0:T(8,128)(2,1)} %bitcast.10, bf16[31,40]{1,0:T(8,128)(2,1)} %bitcast.11, bf16[31,40]{1,0:T(8,128)(2,1)} %bitcast.12, f32[3,1,40]{2,1,0:T(1,128)} %bitcast.13, f32[1,2]{1,0:T(1,128)} %shift_ref.1, s32[1,1]{1,0:T(1,128)} %bitcast.9.visit_ref, bf16[1,4]{1,0:T(2,128)(2,1)} %bitcast.14, ...), custom_call_target="tpu_custom_call" | custom-call | tf_op jit(solution)/shard_map/coadd/pallas_call | solution.py:371
  15.9 0.6 %hand_over.1 = (f32[128,128]{1,0:T(8,128)}, f32[1,128]{1,0:T(1,128)}) custom-call(f32[136,128]{1,0:T(8,128)S(1)} %coadd.1.result_ref), custom_call_target="tpu_custom_call" | custom-call | tf_op jit(solution)/shard_map/hand_over/pallas_call | solution.py:406

commit v4 on v3

--- a/solution.py
+++ b/solution.py
@@ -51,8 +51,6 @@
     offset_ref,
     result_ref,
     xpad,
-    lhs,
-    rhs,
     pick,
     taps2d,
     acc,
@@ -133,14 +131,12 @@
     spill_lanes = lax.div(lane8, jnp.int32(TILE_R)) == lax.rem(me, spill_group)
     header = jnp.where((sub8 == 1) & tile_lanes, weight8, 0.0)
     header = jnp.where((sub8 == 2) & spill_lanes, weight8, header)
-    header = jnp.where(sub8 == 3, covered * weight8, header)
+    header = jnp.where(sub8 == 3, covered, header)
     header = jnp.where(sub8 == 0, targets, header)
-    meta_send[...] = header.reshape(sky, TILE_R, LANES)
+    meta_send[...] = header.reshape(sky, TILE_R, LANES).astype(BF16)
 
     def message(send, recv, ssem, rsem, turn):
-        away = lax.div(turn, 2)
-        step = sky // 2 + jnp.where(lax.rem(turn, 2) == 1, away, -away)
-        to = lax.rem(me + step, sky)
+        to = lax.rem(me + turn, sky)
         return pltpu.make_async_remote_copy(
             src_ref=send.at[to],
             dst_ref=recv.at[me],
@@ -202,8 +198,7 @@
     signed = lax.rem(iota(eight, 1) + LANES // 2, jnp.int32(LANES)) - LANES // 2
     column_pos = (2.0 * signed.astype(F32) + 1.0) / win_cols - 1.0
 
-    def put(block_index, tap):
-        here = pl.ds(block_index * win_cols, win_cols)
+    def toeplitz(tap):
         fixed, slope = (
             pltpu.roll(
                 jnp.broadcast_to(taps2d[term, tap : tap + 1, :], eight),
@@ -220,8 +215,9 @@
             value = fixed + (2.0 * first / win_cols) * slope
             rows.append(pltpu.roll(value, first, 1) if first else value)
         value = jnp.concatenate(rows, axis=0)
-        rhs[here, 0:win_cols] = jnp.where(band, value, 0.0).astype(BF16)
-        rhs[here, win_cols:] = jnp.where(far_band, value, 0.0).astype(BF16)
+        return jnp.concatenate(
+            [jnp.where(band, value, 0.0), jnp.where(far_band, value, 0.0)], axis=1
+        ).astype(BF16)
 
     wide = tiles * TILE_R
     widen = onehot(
@@ -235,30 +231,27 @@
     sent = sky * span
 
     def build(first, last):
+        left, right = [], []
         for tap in range(first, last):
-            put(2 * tap, tap)
-            put(2 * tap + 1, tap + 16)
+            right += [toeplitz(tap), toeplitz(tap + 16)]
             moved = xpad[pl.ds(tap + 16 - half, win_rows + 16), :].astype(BF16)
-            lhs[:, tap * 256 : tap * 256 + 128] = moved[0:win_rows]
-            lhs[:, tap * 256 + 128 : tap * 256 + 256] = moved[16 : win_rows + 16]
+            left += [moved[0:win_rows], moved[16 : win_rows + 16]]
+        return jnp.concatenate(left, axis=1), jnp.concatenate(right, axis=0)
 
     depth = 16 // STEPS
-    build(0, depth)
+    ready = build(0, depth)
     for step in range(STEPS):
         if step + 1 < STEPS:
-            build((step + 1) * depth, (step + 2) * depth)
+            later = build((step + 1) * depth, (step + 2) * depth)
         else:
             pick[0:sent, :] = onehot(iota((sent, wide), 0).astype(F32) == slot_lane)
             pick[sent:, :] = onehot(
                 iota((sky * TILE_R, wide), 0).astype(F32) == spill_lane
             )
-        inner = slice(step * depth * 256, (step + 1) * depth * 256)
-        term = dot(lhs[:, inner], rhs[inner, :])
+        term = dot(*ready)
+        ready = later
         acc[...] = term if step == 0 else acc[...] + term
 
-    pl.semaphore_wait(barrier, sky - 1)
-    lax.fori_loop(1, sky, start_meta, 0)
-    meta_recv[pl.ds(me, 1)] = meta_send[pl.ds(me, 1)]
 
     across = lanczos(shift_ref[0:1, 1:2])
     down = lanczos(shift_ref[0:1, 0:1])
@@ -299,7 +292,10 @@
         message(data_send, data_recv, data_ssem, data_rsem, step).start()
         return carry
 
+    pl.semaphore_wait(barrier, sky - 1)
+    lax.fori_loop(1, sky, start_meta, 0)
     lax.fori_loop(1, sky, start_data, 0)
+    meta_recv[pl.ds(me, 1)] = meta_send[pl.ds(me, 1)]
     data_recv[pl.ds(me, 1)] = data_send[pl.ds(me, 1)]
 
     wait_all(meta_send, meta_recv, meta_ssem, meta_rsem)
@@ -310,9 +306,8 @@
     total = jnp.zeros((owned_rows, win_cols), F32)
     ones = jnp.ones((LANES, win_cols), BF16)
     for group in range(sky // per_group):
-        head = jnp.sum(
-            meta_recv[group * per_group : (group + 1) * per_group], axis=0
-        )
+        head = meta_recv[group * per_group : (group + 1) * per_group]
+        head = jnp.sum(head.astype(F32), axis=0)
         place = jnp.where(head[0:1, :] == row_id, head[1:2, :], 0.0).astype(BF16)
         places.append(place)
         total = total + dot(place, ones)
@@ -321,9 +316,10 @@
     here_row = lax.rem(iota(eight, 1), jnp.int32(TILE_R)) == iota(eight, 0)
     first_rows = jnp.zeros(eight, F32)
     for group in range(sky // spill_group):
-        head = jnp.sum(meta_recv[group * spill_group : (group + 1) * spill_group], axis=0)
+        head = meta_recv[group * spill_group : (group + 1) * spill_group]
+        head = jnp.sum(head.astype(F32), axis=0)
         spill_places.append(jnp.where(same_row, head[2:3, :], 0.0).astype(BF16))
-        count = jnp.sum(jnp.where(here_row, head[3:4, :], 0.0), axis=1, keepdims=True)
+        count = jnp.sum(jnp.where(here_row, head[2:3, :] * head[3:4, :], 0.0), axis=1, keepdims=True)
         first_rows = first_rows + jnp.broadcast_to(count, eight)
     total = total + jnp.concatenate(
         [first_rows, jnp.zeros((owned_rows - TILE_R, LANES), F32)], axis=0
@@ -375,14 +371,12 @@
         out_specs=vmem,
         scratch_shapes=[
             pltpu.VMEM((win_rows + 32, win_cols), F32),
-            pltpu.VMEM((win_rows, 32 * win_cols), BF16),
-            pltpu.VMEM((32 * win_cols, 2 * win_cols), BF16),
             pltpu.VMEM((sky * (span + TILE_R), tiles * TILE_R), BF16),
             pltpu.VMEM((2, 32, LANES), F32),
             pltpu.VMEM((win_rows, 2 * win_cols), F32),
             pltpu.VMEM((win_rows + 16, win_cols), F32),
-            pltpu.VMEM((sky, TILE_R, LANES), F32),
-            pltpu.VMEM((sky, TILE_R, LANES), F32),
+            pltpu.VMEM((sky, TILE_R, LANES), BF16),
+            pltpu.VMEM((sky, TILE_R, LANES), BF16),
             pltpu.VMEM((sky, span + TILE_R, win_cols), BF16),
             pltpu.VMEM((sky, span + TILE_R, win_cols), BF16),
             pltpu.SemaphoreType.DMA,

time: 16.7 us -> 14.9 us (0.89)
  Pallas kernels: 15.3 us -> 13.5 us
    pallas_call x1, Pallas kernels: 14.6 us -> 12.8 us  [on_device(): pl.pallas_call(functools.partial(kernel, sky), out_shape=pltpu.VMEM((owne...]
where the time goes in v4:
time: 14.9 us; the launch traced here: 14.8 us
  Pallas kernels  13.5 us (91%)
  between operations  1.29 us (9%)
    pallas_call x1, Pallas kernels, on_device(): pl.pallas_call(functools.partial(kernel, sky), out_shape=pltpu.VMEM((owne...  12.8 us
    pallas_call x1, Pallas kernels, on_device(): pl.pallas_call(hand_over, out_shape=(jax.ShapeDtypeStruct((owned_rows, wi...  0.64 us

profile of v4, /device:TPU:0, one launch (start us, length us, event | category | flops | bytes accessed | tf_op | source)
XLA Modules:
  0.0 14.8 jit_solution(14285034034078627188)
XLA Ops:
  1.3 12.8 %coadd.1.result_ref = f32[136,128]{1,0:T(8,128)S(1)} custom-call(bf16[512,128]{1,0:T(8,128)(2,1)} %bitcast.10, bf16[31,40]{1,0:T(8,128)(2,1)} %bitcast.11, bf16[31,40]{1,0:T(8,128)(2,1)} %bitcast.12, f32[3,1,40]{2,1,0:T(1,128)} %bitcast.13, f32[1,2]{1,0:T(1,128)} %shift_ref.1, s32[1,1]{1,0:T(1,128)} %bitcast.9.visit_ref, bf16[1,4]{1,0:T(2,128)(2,1)} %bitcast.14, ...), custom_call_target="tpu_custom_call" | custom-call | tf_op jit(solution)/shard_map/coadd/pallas_call | solution.py:367
  14.1 0.6 %hand_over.1 = (f32[128,128]{1,0:T(8,128)}, f32[1,128]{1,0:T(1,128)}) custom-call(f32[136,128]{1,0:T(8,128)S(1)} %coadd.1.result_ref), custom_call_target="tpu_custom_call" | custom-call | tf_op jit(solution)/shard_map/hand_over/pallas_call | solution.py:400
